TPU v7x, 128 devices: a whole 4x4x4 slice. The times are simulated.
128 devices in a mesh: frame: 8 (over z_lo, x), head: 16 (over y, z_hi, core).
Axes of the slice: x: 4, y: 4, z: 4 (z_hi: 2, z_lo: 2; z = z_hi * 2 + z_lo), core: 2. Of those that a mesh axis runs over, the one named last changes fastest.
Arguments:
- tokens: float32 [16, 1024, 1024], P('frame', 'head'), may hold values from -48 to 48
- qkv_weight: float32 [1024, 3072], replicated
- out_weight: float32 [1024, 1024], replicated, may hold values from -0.1875 to 0.1875
- norm_gain: float32 [1024], replicated, may hold values from 0.1 to 1.9
- proj_weight: float32 [1024, 256], replicated, may hold values from -0.1875 to 0.1875
- up_weight: bfloat16 [256, 4096], replicated, may hold values from -0.375 to 0.375
- conv_weight: bfloat16 [2, 3, 3, 256, 256], replicated, may hold values from -0.125 to 0.125
- conv_bias: float32 [2, 256], replicated, may hold values from -3 to 3
- block_lists: int32 [128, 26], P('frame'), may hold values from 0 to 127, as said below
- block_counts: int32 [128], P('frame'), may hold values from 1 to 26, as said below
Outputs:
- refined: bfloat16 [16, 128, 128, 256], P('frame', 'head')
Inputs may be any that keep to these rules, and one draw needn't show every extreme that they name: `block_lists`: row b names 26 different key blocks and its first entry is block b itself; entries at or after the row's count are padding and are ignored. `block_counts`: some query block in every draw has all 26 entries valid.
All inputs are finite; a program needn't handle non-finite values.
Results may differ from a plain program's by a relative error of at most 0.0057.
Values may be sent and summed in bfloat16 or wider, within the bound.
No kernel may reach another device: no remote copies, remote signals or barrier semaphores. Data moves between devices by JAX's collectives and lax.ppermute only.
A program may use at most 128 MiB of HBM per device.

v0:
```python
import functools

import jax
import jax.numpy as jnp
from jax import lax
from jax.experimental import pallas as pl
from jax.experimental.pallas import tpu as pltpu
from jax.sharding import Mesh, PartitionSpec as P

D = 1024
HEADS = 16
HD = 64
CH = 256
SLOTS = 26
STRIP = 64
NEG = -2e38
bf16 = jnp.bfloat16
f32 = jnp.float32


def split(v):
    hi = v.astype(bf16)
    return hi, (v - hi.astype(f32)).astype(bf16)


def dot(a, b):
    return jnp.dot(a, b, preferred_element_type=f32)


def dot3(ah, al, bh, bl):
    m = ah.shape[0]
    both = dot(jnp.concatenate([ah, al], axis=0), bh)
    return both[:m] + (both[m:] + dot(ah, bl))


def lanes(shape):
    return lax.broadcasted_iota(jnp.int32, shape, len(shape) - 1)


def qkv_body(x_ref, w_ref, out_ref, xh, xl):
    @pl.when(pl.program_id(0) == 0)
    def _():
        hi, lo = split(x_ref[...])
        xh[...] = hi
        xl[...] = lo

    wh, wl = split(w_ref[...])
    r = dot3(xh[...], xl[...], wh, wl)
    for u in range(2):
        q = r[:, u * 192 : u * 192 + HD] * 0.125
        k = r[:, u * 192 + HD : u * 192 + 2 * HD]
        v = r[:, u * 192 + 2 * HD : u * 192 + 3 * HD]
        for i, t in enumerate((q, k)):
            lo = t - t.astype(bf16).astype(f32)
            out_ref[u, i * 128 : i * 128 + 128, :] = jnp.concatenate([t, lo], axis=1).astype(bf16)
        out_ref[u, 256:320, :] = jnp.concatenate([v[:STRIP], v[STRIP:]], axis=1).astype(bf16)


def qkv(x, w):
    return pl.pallas_call(
        qkv_body,
        grid=(HEADS // 2,),
        in_specs=[
            pl.BlockSpec((128, D), lambda g: (0, 0)),
            pl.BlockSpec((D, 384), lambda g: (0, g)),
        ],
        out_specs=pl.BlockSpec((2, 320, 128), lambda g: (g, 0, 0)),
        out_shape=jax.ShapeDtypeStruct((HEADS, 320, 128), bf16),
        scratch_shapes=[pltpu.VMEM((128, D), bf16), pltpu.VMEM((128, D), bf16)],
        name="qkv",
    )(x, w)


UNROLL = 8
PAIRS = 16 * (SLOTS // 2)
ROOM = PAIRS + UNROLL


def attend_body(sets, items, cnt, info, kv0, kv1, *refs):
    qrefs, (o_ref, ks, vs, qs, sc, ms, accs) = refs[:-7], refs[-7:]
    low = lanes((128, 128)) < HD

    def strips(ref, j, rows):
        return jnp.concatenate([ref[2 * j, rows, :], ref[2 * j + 1, rows, :]], axis=0)

    def ready(j, _):
        for fr in range(2):
            rows = slice(fr * 64, fr * 64 + 64)
            for src, kv in enumerate((kv0, kv1)):
                b = src * 16 + fr * 8 + j
                a = strips(kv, j, rows).astype(f32)
                swapped = pltpu.roll(a, 64, 1)
                ks[b, :, 0:128] = jnp.where(low, a, swapped).astype(bf16)
                ks[b, :, 128:256] = swapped.astype(bf16)
                v = strips(kv, j, slice(128, 192)).astype(f32)
                if fr:
                    v = pltpu.roll(v, 64, 1)
                vs[b] = jnp.where(low, v, 1.0).astype(bf16)
        return 0

    lax.fori_loop(0, 8, ready, 0)

    for i in range(len(sets)):
        mine = (qrefs[i],) if len(sets) > 1 else qrefs
        for part, q in enumerate(mine):

            def ready_q(j, _, i=i, part=part, q=q):
                for fr in range(2):
                    rows = slice(fr * 64, fr * 64 + 64)
                    qs[17 * i + fr * 8 + 4 * part + j] = strips(q, j, rows)
                return 0

            lax.fori_loop(0, 8 // len(mine), ready_q, 0)
        qs[17 * i + 16] = jnp.zeros((128, 128), bf16)
    vs[32] = jnp.zeros((128, 128), bf16)
    eye = lax.broadcasted_iota(jnp.int32, (128, 128), 0) == lanes((128, 128))

    def one_set(i, _):
        s = sets[0]
        for n in range(1, len(sets)):
            s = jnp.where(i == n, sets[n], s)
        trips = (cnt[s] + UNROLL - 1) // UNROLL

        def clear(b, _):
            ms[b] = jnp.full((128, 128), NEG, f32)
            accs[b] = jnp.zeros((128, 128), f32)
            return 0

        lax.fori_loop(0, 17, clear, 0)

        def score(t, _):
            got = []
            for u in range(UNROLL):
                item = items[s, t * UNROLL + u]
                ia = (item >> 6) & 31
                ib = item & 63
                a = qs[17 * i + (item >> 11)]
                got.append(
                    lax.dot_general(
                        jnp.concatenate([a, a[:, :HD]], axis=1),
                        jnp.concatenate(
                            [ks[ia, :, :192], ks[jnp.where(ib == 32, ia, ib), :, :192]], axis=0
                        ),
                        (((1,), (1,)), ((), ())),
                        preferred_element_type=f32,
                    )
                )
            for u in range(UNROLL):
                qi = items[s, t * UNROLL + u] >> 11
                sc[t * UNROLL + u] = got[u]
                ms[qi] = jnp.maximum(ms[qi], jnp.maximum(got[u][:, :128], got[u][:, 128:]))
            return 0

        lax.fori_loop(0, trips, score, 0)

        def peak(b, _):
            for u in range(4):
                m = jnp.max(ms[4 * b + u], axis=1, keepdims=True)
                ms[4 * b + u] = jnp.broadcast_to(m, (128, 128))
            return 0

        lax.fori_loop(0, 4, peak, 0)

        def blend(t, _):
            got = []
            for u in range(UNROLL):
                item = items[s, t * UNROLL + u]
                m = ms[item >> 11]
                p = jnp.exp(sc[t * UNROLL + u] - jnp.concatenate([m, m], axis=1))
                v = jnp.concatenate([vs[(item >> 6) & 31], vs[item & 63]], axis=0)
                got.append(dot(p.astype(bf16), v))
            for u in range(UNROLL):
                qi = items[s, t * UNROLL + u] >> 11
                accs[qi] = accs[qi] + got[u]
            return 0

        lax.fori_loop(0, trips, blend, 0)
        to = info[s] if len(sets) > 1 else 0

        def diagonal(v):
            return jnp.sum(jnp.where(eye, v, 0.0), axis=0, keepdims=True)

        def emit(jj, _):
            emit_one(2 * jj)
            emit_one(2 * jj + 1)
            return 0

        def emit_one(j):
            a0 = accs[j]
            a1 = accs[8 + j]
            s0 = pltpu.roll(a0, 64, 1)
            s1 = pltpu.roll(a1, 64, 1)
            total = jnp.maximum(jnp.where(low, s0, a1), 0.5)
            out = (jnp.where(low, a0, s1) / total).astype(bf16)
            l0 = jnp.maximum(diagonal(jnp.where(low, s0, a0)), 0.5)
            l1 = jnp.maximum(diagonal(jnp.where(low, s1, a1)), 0.5)
            t0 = diagonal(ms[j]) + jnp.log(l0)
            t1 = diagonal(ms[8 + j]) + jnp.log(l1)
            sub = lax.broadcasted_iota(jnp.int32, (16, 128), 0)
            for half in range(2):
                o_ref[to, 2 * j + half, 0:64, :] = out[half * 64 : half * 64 + 64]
                c = half * 64
                row = jnp.concatenate([t0[:, c : c + 64], t1[:, c : c + 64]], axis=1)
                hi = row.astype(bf16).astype(f32)
                mid = (row - hi).astype(bf16).astype(f32)
                last = row - hi - mid
                tile = jnp.where(
                    sub == 0, hi, jnp.where(sub == 1, mid, jnp.where(sub == 2, last, 0.0))
                )
                o_ref[to, 2 * j + half, 64:80, :] = tile.astype(bf16)

        lax.fori_loop(0, 4, emit, 0)
        return 0

    lax.fori_loop(0, len(sets), one_set, 0)


def attend(sets, items, cnt, info, kv0, kv1, qs):
    smem = pl.BlockSpec(memory_space=pltpu.SMEM)
    vmem = pl.BlockSpec(memory_space=pltpu.VMEM)
    return pl.pallas_call(
        functools.partial(attend_body, sets),
        in_specs=[smem, smem, smem] + [vmem] * (2 + len(qs)),
        out_specs=vmem,
        out_shape=jax.ShapeDtypeStruct((4 if len(sets) > 1 else 1, HEADS, 80, 128), bf16),
        scratch_shapes=[
            pltpu.VMEM((32, 128, 256), bf16),
            pltpu.VMEM((33, 128, 128), bf16),
            pltpu.VMEM((17 * len(sets), 128, 128), bf16),
            pltpu.VMEM((ROOM, 128, 256), f32),
            pltpu.VMEM((17, 128, 128), f32),
            pltpu.VMEM((17, 128, 128), f32),
        ],
        compiler_params=pltpu.CompilerParams(vmem_limit_bytes=44 << 20),
        name=f"attend_{len(sets)}",
    )(items, cnt, info, kv0, kv1, *qs)


def mix_body(r_ref, x_ref, w_ref, gain_ref, proj_ref, feat_ref, top_ref, bot_ref, att):
    lse = jnp.sum(r_ref[:, 64:80, :].astype(f32), axis=1)
    parts = [lse[16 * x : 16 * x + 16] for x in range(4)]
    peak = jnp.maximum(jnp.maximum(parts[0], parts[1]), jnp.maximum(parts[2], parts[3]))
    es = [jnp.exp(p - peak) for p in parts]
    total = (es[0] + es[1]) + (es[2] + es[3])
    share = jnp.concatenate([e / total for e in es], axis=0)
    share = jnp.concatenate([share, share], axis=0).T
    both = jnp.where(lanes((STRIP, 128)) < 64, share[:STRIP], share[STRIP:])
    bh, bl = split(both)
    low = lanes((STRIP, 128)) < HD
    row = lax.broadcasted_iota(jnp.int32, (128, 2048), 0)
    col = lanes((128, 2048))
    half = (row >= 64) == (col % 128 >= 64)
    wide = []
    for x in range(4):
        spread = jnp.where(half & (row % 64 == 16 * x + col // 128), 1.0, 0.0).astype(bf16)
        wide.append(dot(bh, spread) + dot(bl, spread))
    for p in range(HEADS // 2):
        t = []
        for h in (2 * p, 2 * p + 1):
            acc = None
            for x in range(4):
                o = r_ref[16 * x + h, 0:64, :].astype(f32) * wide[x][:, 128 * h : 128 * h + 128]
                acc = o if acc is None else acc + o
            t.append(acc)
        att[0:64, 128 * p : 128 * p + 128] = jnp.where(low, t[0], pltpu.roll(t[1], 64, 1))
        att[64:128, 128 * p : 128 * p + 128] = jnp.where(low, pltpu.roll(t[0], 64, 1), t[1])
    ah, al = split(att[...])
    wh, wl = split(w_ref[...])
    stream = x_ref[...] + dot3(ah, al, wh, wl)
    centred = stream - jnp.mean(stream, axis=1, keepdims=True)
    spread = jnp.mean(centred * centred, axis=1, keepdims=True)
    normed = centred * lax.rsqrt(spread + 1e-05) * gain_ref[...]
    nh, nl = split(normed)
    ph, plo = split(proj_ref[...])
    feat = dot3(nh, nl, ph, plo).astype(bf16)
    feat_ref[...] = feat
    for f in range(2):
        top_ref[32 * f : 32 * f + 32] = feat[64 * f : 64 * f + 32]
        bot_ref[32 * f : 32 * f + 32] = feat[64 * f + 32 : 64 * f + 64]


def mix(r, x, w, gain, proj):
    return pl.pallas_call(
        mix_body,
        out_shape=(
            jax.ShapeDtypeStruct((128, CH), bf16),
            jax.ShapeDtypeStruct((64, CH), bf16),
            jax.ShapeDtypeStruct((64, CH), bf16),
        ),
        scratch_shapes=[pltpu.VMEM((128, D), f32)],
        compiler_params=pltpu.CompilerParams(vmem_limit_bytes=20 << 20),
        name="mix",
    )(r, x, w, gain, proj)


def shifted(dst, src, rows, relu):
    def one(r, _):
        for dx in range(3):
            for half in range(2):
                v = src[half * rows + r, pl.ds(7 + dx, 128), :]
                if relu:
                    v = jnp.maximum(v, 0.0)
                dst[r, :, dx * 256 + half * 128 : dx * 256 + half * 128 + 128] = v.astype(bf16)
        return 0

    lax.fori_loop(0, rows, one, 0)


def head_body(pos, feat_ref, above_ref, below_ref, up_ref, cw_ref, cb_ref, out_ref, ups, u3, hid, h3):
    at = pos[0]

    @pl.when(pl.program_id(0) == 0)
    def _():
        for ref, rows in ((ups, 24), (hid, 20)):
            ref[:, 0:8, :] = jnp.zeros((rows, 8, 128), f32)
            ref[:, 136:144, :] = jnp.zeros((rows, 8, 128), f32)

    own = feat_ref[...]
    early = jnp.concatenate([own, below_ref[...]], axis=0)
    late = jnp.concatenate([above_ref[...], own], axis=0)
    for a in range(4):
        src = early if a < 2 else late
        lifted = dot(src, up_ref[:, 1024 * a : 1024 * a + 1024]).astype(bf16).astype(f32)
        for i in range(3):
            row = 2 + 4 * i + a if a < 2 else 4 * i + a - 2
            for e in range(4):
                for half in range(2):
                    c = 256 * e + 128 * half
                    ups[12 * half + row, pl.ds(8 + e, 32, stride=4), :] = lifted[
                        32 * i : 32 * i + 32, c : c + 128
                    ]
    shifted(u3, ups, 12, True)

    def conv1(r, _):
        acc = None
        for dy in range(3):
            part = dot(u3[pl.ds(2 * r + dy, 2)].reshape(256, 768), cw_ref[0, dy])
            acc = part if acc is None else acc + part
        h = jnp.maximum(acc + cb_ref[0:1, :], 0.0).astype(bf16).astype(f32)
        for k in range(2):
            y = 2 * r + k
            keep = ((y > 0) | (at > 0)) & ((y < 9) | (at < 15))
            v = jnp.where(keep, h[128 * k : 128 * k + 128], 0.0)
            for half in range(2):
                hid[10 * half + y, 8:136, :] = v[:, 128 * half : 128 * half + 128]
        return 0

    lax.fori_loop(0, 5, conv1, 0)
    shifted(h3, hid, 10, False)

    def conv2(r, _):
        acc = None
        for dy in range(3):
            part = dot(h3[pl.ds(2 * r + dy, 2)].reshape(256, 768), cw_ref[1, dy])
            acc = part if acc is None else acc + part
        acc = acc + cb_ref[1:2, :]
        for k in range(2):
            y = 2 * r + k
            for half in range(2):
                c = 128 * half
                v = ups[12 * half + y + 2, 8:136, :] + acc[128 * k : 128 * k + 128, c : c + 128]
                out_ref[0, y, :, c : c + 128] = v.astype(bf16)
        return 0

    lax.fori_loop(0, 4, conv2, 0)


def dense_head(pos, feat, above, below, up, cw, cb):
    whole = lambda shape: pl.BlockSpec(shape, lambda f: (0,) * len(shape))
    return pl.pallas_call(
        head_body,
        grid=(2,),
        in_specs=[
            pl.BlockSpec(memory_space=pltpu.SMEM),
            pl.BlockSpec((64, CH), lambda f: (f, 0)),
            pl.BlockSpec((32, CH), lambda f: (f, 0)),
            pl.BlockSpec((32, CH), lambda f: (f, 0)),
            whole((CH, 16 * CH)),
            whole((2, 3, 3 * CH, CH)),
            whole((2, CH)),
        ],
        out_specs=pl.BlockSpec((1, 8, 128, CH), lambda f: (f, 0, 0, 0)),
        out_shape=jax.ShapeDtypeStruct((2, 8, 128, CH), bf16),
        scratch_shapes=[
            pltpu.VMEM((24, 144, 128), f32),
            pltpu.VMEM((12, 128, 768), bf16),
            pltpu.VMEM((20, 144, 128), f32),
            pltpu.VMEM((10, 128, 768), bf16),
        ],
        compiler_params=pltpu.CompilerParams(vmem_limit_bytes=24 << 20),
        name="dense_head",
    )(pos, feat, above, below, up, cw, cb)


def local_items(lists, counts, x, z):
    packed = jnp.concatenate([lists, counts[:, None]], axis=1)
    sets = [packed] + [
        lax.ppermute(packed, "x", [(i, (i + k) % 4) for i in range(4)]) for k in (1, 2, 3)
    ]
    packed = jnp.stack(sets, axis=0)
    ids = packed[:, :, :SLOTS]
    slot = jnp.arange(SLOTS, dtype=jnp.int32)
    block = jnp.arange(16, dtype=jnp.int32)
    mine = (slot < packed[:, :, SLOTS:]) & ((ids // 16) % 4 == x)
    local = jnp.where(ids // 64 == z, 0, 16) + ids % 16
    ones = mine.astype(jnp.int32)
    inside = jnp.sum(jnp.where(slot[None, :] < slot[:, None], ones[:, :, None, :], 0), axis=-1)
    total = jnp.sum(ones, axis=-1)
    pairs = (total + 1) // 2
    ahead = jnp.sum(jnp.where(block[None, :] < block[:, None], pairs[:, None, :], 0), axis=-1)
    place = jnp.where(mine, ahead[:, :, None] + inside // 2, -1).reshape(4, 1, -1)
    alone = jnp.where(inside + 1 == total[:, :, None], 32, 0)
    value = jnp.where(inside % 2 == 0, block[:, None] * 2048 + local * 64 + alone, local)
    at = jnp.arange(ROOM, dtype=jnp.int32)[:, None]
    items = jnp.sum(jnp.where(place == at, value.reshape(4, 1, -1), 0), axis=-1)
    count = jnp.sum(pairs, axis=-1)
    items = jnp.where(at[:, 0] < count[:, None], items, 16 * 2048 + 32)
    return items, count


def on_device(tokens, qkv_w, out_w, gain, proj_w, up_w, conv_w, conv_b, lists, counts):
    x = lax.axis_index("x")
    z = lax.axis_index("z")
    strip = lax.axis_index("head")
    flat = tokens.reshape(-1, D)
    right = [(i, (i + 1) % 4) for i in range(4)]
    left = [(i, (i - 1) % 4) for i in range(4)]
    packed = qkv(flat, qkv_w)
    packed, lists, counts = lax.optimization_barrier((packed, lists, counts))
    items, cnt = local_items(lists, counts, x, z)
    packed = lax.all_to_all(packed, "head", split_axis=0, concat_axis=0, tiled=True)
    q = packed[:, :128]
    kv = packed[:, 128:]
    q1 = lax.ppermute(q, "x", right)
    q3 = lax.ppermute(q, "x", left)
    kv_far = lax.ppermute(kv, "z", [(0, 1), (1, 0)])
    q2a = lax.ppermute(q1[:8], "x", right)
    q2b = lax.ppermute(q3[8:], "x", left)
    info = (x - jnp.arange(4, dtype=jnp.int32)) % 4
    part = attend((0, 1, 3), items, cnt, info, kv, kv_far, [q, q1, q3])
    last = attend((2,), items, cnt, info, kv, kv_far, [q2a, q2b])
    part = lax.dynamic_update_slice_in_dim(part, last, info[2], 0)
    part = lax.all_to_all(
        part.reshape(64, 80, 128), ("x", "head"), split_axis=0, concat_axis=0, tiled=True
    )
    feat, top, bot = mix(part, flat, out_w, gain[None, :], proj_w)
    above = lax.ppermute(bot, "head", [(i, i + 1) for i in range(15)])
    below = lax.ppermute(top, "head", [(i + 1, i) for i in range(15)])
    return dense_head(
        strip[None], feat, above, below, up_w, conv_w.reshape(2, 3, 3 * CH, CH), conv_b
    )


def solution(mesh):
    grid = Mesh(mesh.devices.reshape(2, 4, 16), ("z", "x", "head"))
    rows = ("z", "x")
    in_specs = (
        P(rows, "head", None),
        P(),
        P(),
        P(),
        P(),
        P(),
        P(),
        P(),
        P(rows, None),
        P(rows),
    )
    return jax.shard_map(
        on_device,
        mesh=grid,
        in_specs=in_specs,
        out_specs=P(rows, "head", None, None),
        check_vma=False,
    )
```

profile of v0, /device:TPU:1, one launch (start us, length us, event | category | flops | bytes accessed | tf_op | source)
XLA Modules:
  0.0 142.1 jit_solution(10148682791321176661)
XLA Ops:
  0.0 10.4 %qkv.1 = bf16[16,320,128]{2,1,0:T(8,128)(2,1)} custom-call(f32[128,1024]{1,0:T(8,128)} %bitcast.15, f32[1024,3072]{1,0:T(8,128)} %w_ref.2), custom_call_target="tpu_custom_call" | custom-call | tf_op jit(solution)/shard_map/qkv/pallas_call | solution.py:60
  10.4 9.4 %all-to-all-start = ((bf16[16,320,128]{2,1,0:T(8,128)(2,1)}), bf16[16,320,128]{2,1,0:T(8,128)(2,1)S(1)}, u32[]{:S(2)}, u32[]{:S(2)}) async-start(bf16[16,320,128]{2,1,0:T(8,128)(2,1)} %qkv.1), calls=%async_computation | async-start | bytes 2621440 | tf_op jit(solution)/shard_map/all_to_all | solution.py:431
  19.9 2.5 %collective-permute-start.2 = (s32[16,27]{0,1:T(8,128)S(1)}, s32[16,27]{0,1:T(8,128)S(1)}, u32[]{:S(2)}, u32[]{:S(2)}) collective-permute-start(s32[16,27]{0,1:T(8,128)S(1)} %pad_add_fusion.3), channel_id=1, source_target_pairs={{0,48},{16,0},{32,16},{48,32},{1,49},{17,1},{33,17},{49,33},{2,50}... | collective-permute-start | bytes 5192 | tf_op jit(solution)/shard_map/ppermute | solution.py:398
  23.0 0.6 collective-permute-start
  26.2 0.7 collective-permute-done.1
  27.2 12.5 %all-to-all-done = bf16[16,320,128]{2,1,0:T(8,128)(2,1)S(1)} async-done(((bf16[16,320,128]{2,1,0:T(8,128)(2,1)}), bf16[16,320,128]{2,1,0:T(8,128)(2,1)S(1)}, u32[]{:S(2)}, u32[]{:S(2)}) %all-to-all-start) | async-done | bytes 1310752 | tf_op jit(solution)/shard_map/all_to_all | solution.py:431
  39.7 1.1 copy-done.7
  40.8 1.3 collective-permute-start.4
  42.1 1.5 %collective-permute-start.5 = (bf16[16,128,128]{2,1,0:T(8,128)(2,1)S(1)}, bf16[16,128,128]{2,1,0:T(8,128)(2,1)S(1)}, u32[]{:S(2)}, u32[]{:S(2)}) collective-permute-start(bf16[16,128,128]{2,1,0:T(8,128)(2,1)S(1)} %slice.29.refs_0_), channel_id=1, source_target_pairs={{0,48},{16,0},{32,16},{48,32},{1,49},{17,1},{33,17},{49,33},{2,50}... | collective-permute-start | bytes 1572872 | tf_op jit(solution)/shard_map/ppermute | solution.py:435
  43.7 1.2 slice.28.kv0
  44.9 0.8 collective-permute-start.3
  46.0 1.8 %select_reduce_fusion.1 = s32[4,16,26]{1,2,0:T(8,128)S(1)} fusion(s32[4,16,26]{2,1,0:T(8,128)S(1)} %copy.16, pred[26,26]{1,0:T(8,128)(4,1)S(1)} %iota_compare_fusion.2), kind=kLoop, calls=%fused_computation.2 | loop fusion | flops 84864 | bytes 13988 | tf_op jit(solution)/shard_map/reduce_sum | solution.py:407
  48.3 6.3 %collective-permute-done.4.refs_1_ = bf16[16,128,128]{2,1,0:T(8,128)(2,1)S(1)} collective-permute-done((bf16[16,128,128]{2,1,0:T(8,128)(2,1)S(1)}, bf16[16,128,128]{2,1,0:T(8,128)(2,1)S(1)}, u32[]{:S(2)}, u32[]{:S(2)}) %collective-permute-start.4) | collective-permute-done | bytes 524320 | tf_op jit(solution)/shard_map/ppermute | solution.py:434
  54.8 2.7 %collective-permute-start.7 = (bf16[8,128,128]{2,1,0:T(8,128)(2,1)S(1)}, bf16[8,128,128]{2,1,0:T(8,128)(2,1)S(1)}, u32[]{:S(2)}, u32[]{:S(2)}) collective-permute-start(bf16[8,128,128]{2,1,0:T(8,128)(2,1)S(1)} %slice.31), channel_id=1, source_target_pairs={{0,48},{16,0},{32,16},{48,32},{1,49},{17,1},{33,17},{49,33},{2,50}... | collective-permute-start | bytes 786440 | tf_op jit(solution)/shard_map/ppermute | solution.py:438
  58.2 4.4 %collective-permute-done.3.kv1 = bf16[16,192,128]{2,1,0:T(8,128)(2,1)S(1)} collective-permute-done((bf16[16,192,128]{2,1,0:T(8,128)(2,1)S(1)}, bf16[16,192,128]{2,1,0:T(8,128)(2,1)S(1)}, u32[]{:S(2)}, u32[]{:S(2)}) %collective-permute-start.3) | collective-permute-done | bytes 786464 | tf_op jit(solution)/shard_map/ppermute | solution.py:436
  62.5 15.3 %attend_3.1 = bf16[4,16,80,128]{3,2,1,0:T(8,128)(2,1)S(1)} custom-call(s32[4,216]{1,0:T(4,128)S(1)} %fusion.13.items, s32[4]{0:T(128)S(1)} %get-tuple-element.17.cnt, s32[4]{0:T(128)S(1)} %and_select_fusion.info, bf16[16,192,128]{2,1,0:T(8,128)(2,1)S(1)} %slice.28.kv0, bf16[16,192,128]{2,1,0:T(8,128)(2,1)S(1)} %collective-permute-done.3.kv1, ...), custom_call_target="tpu_custom_call" | custom-call | tf_op jit(solution)/shard_map/attend_3/pallas_call | solution.py:221
  77.8 9.1 %attend_1.1 = bf16[1,16,80,128]{3,2,1,0:T(8,128)(2,1)S(1)} custom-call(s32[4,216]{1,0:T(4,128)S(1)} %fusion.13.items, s32[4]{0:T(128)S(1)} %get-tuple-element.17.cnt, s32[4]{0:T(128)S(1)} %and_select_fusion.info, bf16[16,192,128]{2,1,0:T(8,128)(2,1)S(1)} %slice.28.kv0, bf16[16,192,128]{2,1,0:T(8,128)(2,1)S(1)} %collective-permute-done.3.kv1, ...), custom_call_target="tpu_custom_call" | custom-call | tf_op jit(solution)/shard_map/attend_1/pallas_call | solution.py:221
  87.1 29.7 %all_to_all.10.r_ref = bf16[64,80,128]{2,1,0:T(8,128)(2,1)S(1)} all-to-all(bf16[64,80,128]{2,1,0:T(8,128)(2,1)S(1)} %bitcast.13), channel_id=1, replica_groups=mesh['z'=2,'x'=4,'head'=16] {'x','head'}, dimensions={0} | all-to-all | bytes 2621440 | tf_op jit(solution)/shard_map/all_to_all | solution.py:443
  116.8 2.8 %mix.1 = (bf16[128,256]{1,0:T(8,128)(2,1)S(1)}, bf16[64,256]{1,0:T(8,128)(2,1)S(1)}, bf16[64,256]{1,0:T(8,128)(2,1)S(1)}) custom-call(bf16[64,80,128]{2,1,0:T(8,128)(2,1)S(1)} %all_to_all.10.r_ref, f32[128,1024]{1,0:T(8,128)S(1)} %bitcast.16, f32[1024,1024]{1,0:T(8,128)S(1)} %copy-done, f32[1,1024]{1,0:T(1,128)S(1)} %bitcast.17, f32[1024,256]{1,0:T(8,128)S(1)} %copy-done.4), custom_call_target="tpu_custom_call" | custom-call | tf_op jit(solution)/shard_map/mix/pallas_call | solution.py:283
  119.6 2.2 %collective-permute-start.8 = (bf16[64,256]{1,0:T(8,128)(2,1)S(1)}, bf16[64,256]{1,0:T(8,128)(2,1)S(1)}, u32[]{:S(2)}, u32[]{:S(2)}) collective-permute-start(bf16[64,256]{1,0:T(8,128)(2,1)S(1)} %get-tuple-element.15), channel_id=1, source_target_pairs={{0,1},{1,2},{2,3},{3,4},{4,5},{5,6},{6,7},{7,8},{8,9},{9,10},{10,1... | collective-permute-start | bytes 98312 | tf_op jit(solution)/shard_map/ppermute | solution.py:447
  121.8 2.1 %collective-permute-start.9 = (bf16[64,256]{1,0:T(8,128)(2,1)S(1)}, bf16[64,256]{1,0:T(8,128)(2,1)S(1)}, u32[]{:S(2)}, u32[]{:S(2)}) collective-permute-start(bf16[64,256]{1,0:T(8,128)(2,1)S(1)} %get-tuple-element.16), channel_id=1, source_target_pairs={{1,0},{2,1},{3,2},{4,3},{5,4},{6,5},{7,6},{8,7},{9,8},{10,9},{11,1... | collective-permute-start | bytes 98312 | tf_op jit(solution)/shard_map/ppermute | solution.py:448
  123.9 4.6 %collective-permute-done.9.below_ref = bf16[64,256]{1,0:T(8,128)(2,1)S(1)} collective-permute-done((bf16[64,256]{1,0:T(8,128)(2,1)S(1)}, bf16[64,256]{1,0:T(8,128)(2,1)S(1)}, u32[]{:S(2)}, u32[]{:S(2)}) %collective-permute-start.9) | collective-permute-done | bytes 32800 | tf_op jit(solution)/shard_map/ppermute | solution.py:448
  128.5 1.6 %copy-done.3 = bf16[256,4096]{1,0:T(8,128)(2,1)S(1)} copy-done((bf16[256,4096]{1,0:T(8,128)(2,1)S(1)}, bf16[256,4096]{1,0:T(8,128)(2,1)}, u32[]{:S(2)}) %copy-start.3) | copy-done | bytes 2097176
  130.1 12.0 %dense_head.1 = bf16[2,8,128,256]{3,2,1,0:T(8,128)(2,1)} custom-call(s32[1]{0:T(128)} %bitcast.pos, bf16[128,256]{1,0:T(8,128)(2,1)S(1)} %get-tuple-element.14.feat_ref, bf16[64,256]{1,0:T(8,128)(2,1)S(1)} %collective-permute-done.8.above_ref, bf16[64,256]{1,0:T(8,128)(2,1)S(1)} %collective-permute-done.9.below_ref, bf16[256,4096]{1,0:T(8,128)(2,1)S(1)} %copy-done.3, ...), custom_call_target="tpu_custom_call" | custom-call | tf_op jit(solution)/shard_map/dense_head/pallas_call | solution.py:370
  (51 shorter events, 3.4 us)
Async XLA Ops:
  10.4 9.4 %copy-start.8 = (s32[16,26]{1,0:T(8,128)S(1)}, s32[16,26]{1,0:T(8,128)}, u32[]{:S(2)}) copy-start(s32[16,26]{1,0:T(8,128)} %param.18) | copy-start | bytes 4996
  10.4 9.5 %copy-start.9 = (s32[16]{0:T(128)S(1)}, s32[16]{0:T(128)}, u32[]{:S(2)}) copy-start(s32[16]{0:T(128)} %param.19) | copy-start | bytes 196
  10.4 29.3 %all-to-all-start = ((bf16[16,320,128]{2,1,0:T(8,128)(2,1)}), bf16[16,320,128]{2,1,0:T(8,128)(2,1)S(1)}, u32[]{:S(2)}, u32[]{:S(2)}) async-start(bf16[16,320,128]{2,1,0:T(8,128)(2,1)} %qkv.1), calls=%async_computation | async-start | bytes 2621440 | tf_op jit(solution)/shard_map/all_to_all | solution.py:431
  19.9 6.3 %collective-permute-start.2 = (s32[16,27]{0,1:T(8,128)S(1)}, s32[16,27]{0,1:T(8,128)S(1)}, u32[]{:S(2)}, u32[]{:S(2)}) collective-permute-start(s32[16,27]{0,1:T(8,128)S(1)} %pad_add_fusion.3), channel_id=1, source_target_pairs={{0,48},{16,0},{32,16},{48,32},{1,49},{17,1},{33,17},{49,33},{2,50}... | collective-permute-start | bytes 5192 | tf_op jit(solution)/shard_map/ppermute | solution.py:398
  22.5 4.4 %collective-permute-start.1 = (s32[16,27]{0,1:T(8,128)S(1)}, s32[16,27]{0,1:T(8,128)S(1)}, u32[]{:S(2)}, u32[]{:S(2)}) collective-permute-start(s32[16,27]{0,1:T(8,128)S(1)} %pad_add_fusion.3), channel_id=1, source_target_pairs={{0,32},{16,48},{32,0},{48,16},{1,33},{17,49},{33,1},{49,17},{2,34}... | collective-permute-start | bytes 5192 | tf_op jit(solution)/shard_map/ppermute | solution.py:398
  23.0 4.1 %collective-permute-start = (s32[16,27]{0,1:T(8,128)S(1)}, s32[16,27]{0,1:T(8,128)S(1)}, u32[]{:S(2)}, u32[]{:S(2)}) collective-permute-start(s32[16,27]{0,1:T(8,128)S(1)} %pad_add_fusion.3), channel_id=1, source_target_pairs={{0,16},{16,32},{32,48},{48,0},{1,17},{17,33},{33,49},{49,1},{2,18}... | collective-permute-start | bytes 5192 | tf_op jit(solution)/shard_map/ppermute | solution.py:398
  39.7 1.1 copy-start.7
  40.8 13.8 %collective-permute-start.4 = (bf16[16,128,128]{2,1,0:T(8,128)(2,1)S(1)}, bf16[16,128,128]{2,1,0:T(8,128)(2,1)S(1)}, u32[]{:S(2)}, u32[]{:S(2)}) collective-permute-start(bf16[16,128,128]{2,1,0:T(8,128)(2,1)S(1)} %slice.29.refs_0_), channel_id=1, source_target_pairs={{0,16},{16,32},{32,48},{48,0},{1,17},{17,33},{33,49},{49,1},{2,18}... | collective-permute-start | bytes 1572872 | tf_op jit(solution)/shard_map/ppermute | solution.py:434
  42.1 12.6 %collective-permute-start.5 = (bf16[16,128,128]{2,1,0:T(8,128)(2,1)S(1)}, bf16[16,128,128]{2,1,0:T(8,128)(2,1)S(1)}, u32[]{:S(2)}, u32[]{:S(2)}) collective-permute-start(bf16[16,128,128]{2,1,0:T(8,128)(2,1)S(1)} %slice.29.refs_0_), channel_id=1, source_target_pairs={{0,48},{16,0},{32,16},{48,32},{1,49},{17,1},{33,17},{49,33},{2,50}... | collective-permute-start | bytes 1572872 | tf_op jit(solution)/shard_map/ppermute | solution.py:435
  44.9 17.7 %collective-permute-start.3 = (bf16[16,192,128]{2,1,0:T(8,128)(2,1)S(1)}, bf16[16,192,128]{2,1,0:T(8,128)(2,1)S(1)}, u32[]{:S(2)}, u32[]{:S(2)}) collective-permute-start(bf16[16,192,128]{2,1,0:T(8,128)(2,1)S(1)} %slice.28.kv0), channel_id=1, source_target_pairs={{0,64},{64,0},{1,65},{65,1},{2,66},{66,2},{3,67},{67,3},{4,68},{68... | collective-permute-start | bytes 2359304 | tf_op jit(solution)/shard_map/ppermute | solution.py:436
  54.6 23.2 %collective-permute-start.6 = (bf16[8,128,128]{2,1,0:T(8,128)(2,1)S(1)}, bf16[8,128,128]{2,1,0:T(8,128)(2,1)S(1)}, u32[]{:S(2)}, u32[]{:S(2)}) collective-permute-start(bf16[8,128,128]{2,1,0:T(8,128)(2,1)S(1)} %slice.30), channel_id=1, source_target_pairs={{0,16},{16,32},{32,48},{48,0},{1,17},{17,33},{33,49},{49,1},{2,18}... | collective-permute-start | bytes 786440 | tf_op jit(solution)/shard_map/ppermute | solution.py:437
  54.8 23.1 %collective-permute-start.7 = (bf16[8,128,128]{2,1,0:T(8,128)(2,1)S(1)}, bf16[8,128,128]{2,1,0:T(8,128)(2,1)S(1)}, u32[]{:S(2)}, u32[]{:S(2)}) collective-permute-start(bf16[8,128,128]{2,1,0:T(8,128)(2,1)S(1)} %slice.31), channel_id=1, source_target_pairs={{0,48},{16,0},{32,16},{48,32},{1,49},{17,1},{33,17},{49,33},{2,50}... | collective-permute-start | bytes 786440 | tf_op jit(solution)/shard_map/ppermute | solution.py:438
  62.5 54.2 %copy-start.4 = (f32[1024,256]{1,0:T(8,128)S(1)}, f32[1024,256]{1,0:T(8,128)}, u32[]{:S(2)}) copy-start(f32[1024,256]{1,0:T(8,128)} %proj_ref.1) | copy-start | bytes 3145732
  77.8 38.9 %copy-start = (f32[1024,1024]{1,0:T(8,128)S(1)}, f32[1024,1024]{1,0:T(8,128)}, u32[]{:S(2)}) copy-start(f32[1024,1024]{1,0:T(8,128)} %w_ref.3) | copy-start | bytes 12582916
  87.0 29.8 %copy-start.2 = (f32[2,64,1024]{2,1,0:T(8,128)S(1)}, f32[2,64,1024]{2,1,0:T(8,128)}, u32[]{:S(2)}) copy-start(f32[2,64,1024]{2,1,0:T(8,128)} %param.10) | copy-start | bytes 1572868
  87.0 29.8 %copy-start.5 = (f32[1024]{0:T(1024)S(1)}, f32[1024]{0:T(1024)}, u32[]{:S(2)}) copy-start(f32[1024]{0:T(1024)} %param.13) | copy-start | bytes 12292
  116.8 11.8 %copy-start.1 = (bf16[2,3,3,256,256]{4,3,2,1,0:T(8,128)(2,1)S(1)}, bf16[2,3,3,256,256]{4,3,2,1,0:T(8,128)(2,1)}, u32[]{:S(2)}) copy-start(bf16[2,3,3,256,256]{4,3,2,1,0:T(8,128)(2,1)} %param.16) | copy-start | bytes 7077892
  116.8 11.8 %copy-start.6 = (f32[2,256]{1,0:T(2,128)S(1)}, f32[2,256]{1,0:T(2,128)}, u32[]{:S(2)}) copy-start(f32[2,256]{1,0:T(2,128)} %cb_ref.1) | copy-start | bytes 6148
  119.6 4.3 %collective-permute-start.8 = (bf16[64,256]{1,0:T(8,128)(2,1)S(1)}, bf16[64,256]{1,0:T(8,128)(2,1)S(1)}, u32[]{:S(2)}, u32[]{:S(2)}) collective-permute-start(bf16[64,256]{1,0:T(8,128)(2,1)S(1)} %get-tuple-element.15), channel_id=1, source_target_pairs={{0,1},{1,2},{2,3},{3,4},{4,5},{5,6},{6,7},{7,8},{8,9},{9,10},{10,1... | collective-permute-start | bytes 98312 | tf_op jit(solution)/shard_map/ppermute | solution.py:447
  121.8 6.7 %collective-permute-start.9 = (bf16[64,256]{1,0:T(8,128)(2,1)S(1)}, bf16[64,256]{1,0:T(8,128)(2,1)S(1)}, u32[]{:S(2)}, u32[]{:S(2)}) collective-permute-start(bf16[64,256]{1,0:T(8,128)(2,1)S(1)} %get-tuple-element.16), channel_id=1, source_target_pairs={{1,0},{2,1},{3,2},{4,3},{5,4},{6,5},{7,6},{8,7},{9,8},{10,9},{11,1... | collective-permute-start | bytes 98312 | tf_op jit(solution)/shard_map/ppermute | solution.py:448
  128.5 1.6 %copy-start.3 = (bf16[256,4096]{1,0:T(8,128)(2,1)S(1)}, bf16[256,4096]{1,0:T(8,128)(2,1)}, u32[]{:S(2)}) copy-start(bf16[256,4096]{1,0:T(8,128)(2,1)} %up_ref.1) | copy-start | bytes 6291460
where the time goes:
time: 143 us; the launch traced here: 142 us
  Pallas kernels  49.5 us (35%)
  blocking collectives  29.7 us (21%)
  waiting for transfers between devices  28.7 us (20%)
  starting transfers between devices  23.8 us (17%)
  local copies, waits for them, and re-layouts  5.17 us (4%)
  other arithmetic  3.09 us (2%)
  between operations  2.19 us (2%)
    all_to_all x1, blocking collectives, on_device(): lax.all_to_all(part.reshape(64, 80, 128), ('x', 'head'), split_axis=0, co...  29.7 us
    pallas_call x2, Pallas kernels, attend(): pl.pallas_call(functools.partial(attend_body, sets), in_specs=[smem, smem...  24.4 us
    all_to_all x1, waiting for transfers between devices, on_device(): lax.all_to_all(packed, 'head', split_axis=0, concat_axis=0, tiled=True)  12.5 us
    pallas_call x1, Pallas kernels, dense_head(): pl.pallas_call(head_body, grid=(2,), in_specs=[pl.BlockSpec(memory_space=...  12 us
    pallas_call x1, Pallas kernels, qkv(): pl.pallas_call(qkv_body, grid=(HEADS // 2,), in_specs=[pl.BlockSpec((128,...  10.4 us
    all_to_all x1, starting transfers between devices, on_device(): lax.all_to_all(packed, 'head', split_axis=0, concat_axis=0, tiled=True)  9.42 us
    ppermute x1, waiting for transfers between devices, on_device(): q1 = lax.ppermute(q, 'x', right)  6.28 us
    ppermute x1, waiting for transfers between devices, on_device(): below = lax.ppermute(top, 'head', [(i + 1, i) for i in range(15)])  4.58 us
  transfers between devices with their start and end apart: 11, of which 6 were waited for; matrix products, arithmetic and copies ran while one was open for 4% of the time, Pallas kernels for 11%

commit v1 on v0

--- a/solution.py
+++ b/solution.py
@@ -115,18 +115,18 @@
     vs[32] = jnp.zeros((128, 128), bf16)
     eye = lax.broadcasted_iota(jnp.int32, (128, 128), 0) == lanes((128, 128))
 
+    def clear(b, _):
+        ms[b] = jnp.full((128, 128), NEG, f32)
+        return 0
+
+    lax.fori_loop(0, 17, clear, 0)
+    accs[16] = jnp.zeros((128, 128), f32)
+
     def one_set(i, _):
         s = sets[0]
         for n in range(1, len(sets)):
             s = jnp.where(i == n, sets[n], s)
         trips = (cnt[s] + UNROLL - 1) // UNROLL
-
-        def clear(b, _):
-            ms[b] = jnp.full((128, 128), NEG, f32)
-            accs[b] = jnp.zeros((128, 128), f32)
-            return 0
-
-        lax.fori_loop(0, 17, clear, 0)
 
         def score(t, _):
             got = []
@@ -154,12 +154,13 @@
         lax.fori_loop(0, trips, score, 0)
 
         def peak(b, _):
-            for u in range(4):
-                m = jnp.max(ms[4 * b + u], axis=1, keepdims=True)
-                ms[4 * b + u] = jnp.broadcast_to(m, (128, 128))
+            for u in range(8):
+                m = jnp.max(ms[8 * b + u], axis=1, keepdims=True)
+                ms[8 * b + u] = jnp.broadcast_to(m, (128, 128))
+                accs[8 * b + u] = jnp.zeros((128, 128), f32)
             return 0
 
-        lax.fori_loop(0, 4, peak, 0)
+        lax.fori_loop(0, 2, peak, 0)
 
         def blend(t, _):
             got = []
@@ -196,7 +197,9 @@
             l1 = jnp.maximum(diagonal(jnp.where(low, s1, a1)), 0.5)
             t0 = diagonal(ms[j]) + jnp.log(l0)
             t1 = diagonal(ms[8 + j]) + jnp.log(l1)
-            sub = lax.broadcasted_iota(jnp.int32, (16, 128), 0)
+            ms[j] = jnp.full((128, 128), NEG, f32)
+            ms[8 + j] = jnp.full((128, 128), NEG, f32)
+            sub = lax.broadcasted_iota(jnp.int32, (8, 128), 0)
             for half in range(2):
                 o_ref[to, 2 * j + half, 0:64, :] = out[half * 64 : half * 64 + 64]
                 c = half * 64
@@ -207,7 +210,7 @@
                 tile = jnp.where(
                     sub == 0, hi, jnp.where(sub == 1, mid, jnp.where(sub == 2, last, 0.0))
                 )
-                o_ref[to, 2 * j + half, 64:80, :] = tile.astype(bf16)
+                o_ref[to, 2 * j + half, 64:72, :] = tile.astype(bf16)
 
         lax.fori_loop(0, 4, emit, 0)
         return 0
@@ -222,7 +225,7 @@
         functools.partial(attend_body, sets),
         in_specs=[smem, smem, smem] + [vmem] * (2 + len(qs)),
         out_specs=vmem,
-        out_shape=jax.ShapeDtypeStruct((4 if len(sets) > 1 else 1, HEADS, 80, 128), bf16),
+        out_shape=jax.ShapeDtypeStruct((4 if len(sets) > 1 else 1, HEADS, 72, 128), bf16),
         scratch_shapes=[
             pltpu.VMEM((32, 128, 256), bf16),
             pltpu.VMEM((33, 128, 128), bf16),
@@ -231,13 +234,12 @@
             pltpu.VMEM((17, 128, 128), f32),
             pltpu.VMEM((17, 128, 128), f32),
         ],
-        compiler_params=pltpu.CompilerParams(vmem_limit_bytes=44 << 20),
-        name=f"attend_{len(sets)}",
+        compiler_params=pltpu.CompilerParams(vmem_limit_bytes=38 << 20),
     )(items, cnt, info, kv0, kv1, *qs)
 
 
 def mix_body(r_ref, x_ref, w_ref, gain_ref, proj_ref, feat_ref, top_ref, bot_ref, att):
-    lse = jnp.sum(r_ref[:, 64:80, :].astype(f32), axis=1)
+    lse = jnp.sum(r_ref[:, 64:72, :].astype(f32), axis=1)
     parts = [lse[16 * x : 16 * x + 16] for x in range(4)]
     peak = jnp.maximum(jnp.maximum(parts[0], parts[1]), jnp.maximum(parts[2], parts[3]))
     es = [jnp.exp(p - peak) for p in parts]
@@ -431,9 +433,9 @@
     packed = lax.all_to_all(packed, "head", split_axis=0, concat_axis=0, tiled=True)
     q = packed[:, :128]
     kv = packed[:, 128:]
+    kv_far = lax.ppermute(kv, "z", [(0, 1), (1, 0)])
     q1 = lax.ppermute(q, "x", right)
     q3 = lax.ppermute(q, "x", left)
-    kv_far = lax.ppermute(kv, "z", [(0, 1), (1, 0)])
     q2a = lax.ppermute(q1[:8], "x", right)
     q2b = lax.ppermute(q3[8:], "x", left)
     info = (x - jnp.arange(4, dtype=jnp.int32)) % 4
@@ -441,7 +443,7 @@
     last = attend((2,), items, cnt, info, kv, kv_far, [q2a, q2b])
     part = lax.dynamic_update_slice_in_dim(part, last, info[2], 0)
     part = lax.all_to_all(
-        part.reshape(64, 80, 128), ("x", "head"), split_axis=0, concat_axis=0, tiled=True
+        part.reshape(64, 72, 128), ("x", "head"), split_axis=0, concat_axis=0, tiled=True
     )
     feat, top, bot = mix(part, flat, out_w, gain[None, :], proj_w)
     above = lax.ppermute(bot, "head", [(i, i + 1) for i in range(15)])

time: 143 us -> 141 us (0.986)
  the two profiles are of different devices: /device:TPU:1 before, /device:TPU:97 now
where the time goes in v1:
time: 141 us; the launch traced here: 140 us
  Pallas kernels  48.7 us (35%)
  waiting for transfers between devices  29.6 us (21%)
  blocking collectives  26.2 us (19%)
  starting transfers between devices  25.3 us (18%)
  local copies, waits for them, and re-layouts  5.17 us (4%)
  other arithmetic  3.09 us (2%)
  between operations  2.19 us (2%)
    all_to_all x1, blocking collectives, on_device(): lax.all_to_all(part.reshape(64, 72, 128), ('x', 'head'), split_axis=0, co...  26.2 us
    pallas_call x2, Pallas kernels, attend(): pl.pallas_call(functools.partial(attend_body, sets), in_specs=[smem, smem...  23.6 us
    pallas_call x1, Pallas kernels, dense_head(): pl.pallas_call(head_body, grid=(2,), in_specs=[pl.BlockSpec(memory_space=...  12 us
    all_to_all x1, waiting for transfers between devices, on_device(): lax.all_to_all(packed, 'head', split_axis=0, concat_axis=0, tiled=True)  10.8 us
    pallas_call x1, Pallas kernels, qkv(): pl.pallas_call(qkv_body, grid=(HEADS // 2,), in_specs=[pl.BlockSpec((128,...  10.4 us
    all_to_all x1, starting transfers between devices, on_device(): lax.all_to_all(packed, 'head', split_axis=0, concat_axis=0, tiled=True)  7.86 us
    ppermute x1, waiting for transfers between devices, on_device(): q1 = lax.ppermute(q, 'x', right)  7.75 us
    ppermute x1, starting transfers between devices, on_device(): above = lax.ppermute(bot, 'head', [(i, i + 1) for i in range(15)])  6.13 us
  transfers between devices with their start and end apart: 11, of which 6 were waited for; matrix products, arithmetic and copies ran while one was open for 4% of the time, Pallas kernels for 12%

profile of v1, /device:TPU:97, one launch (start us, length us, event | category | flops | bytes accessed | tf_op | source)
XLA Modules:
  0.0 140.3 jit_solution(5126932783922016794)
XLA Ops:
  0.0 10.4 %qkv.1 = bf16[16,320,128]{2,1,0:T(8,128)(2,1)} custom-call(f32[128,1024]{1,0:T(8,128)} %bitcast.15, f32[1024,3072]{1,0:T(8,128)} %w_ref.2), custom_call_target="tpu_custom_call" | custom-call | tf_op jit(solution)/shard_map/qkv/pallas_call | solution.py:60
  10.4 7.9 %all-to-all-start = ((bf16[16,320,128]{2,1,0:T(8,128)(2,1)}), bf16[16,320,128]{2,1,0:T(8,128)(2,1)S(1)}, u32[]{:S(2)}, u32[]{:S(2)}) async-start(bf16[16,320,128]{2,1,0:T(8,128)(2,1)} %qkv.1), calls=%async_computation | async-start | bytes 2621440 | tf_op jit(solution)/shard_map/all_to_all | solution.py:433
  18.4 2.5 %collective-permute-start.2 = (s32[16,27]{0,1:T(8,128)S(1)}, s32[16,27]{0,1:T(8,128)S(1)}, u32[]{:S(2)}, u32[]{:S(2)}) collective-permute-start(s32[16,27]{0,1:T(8,128)S(1)} %pad_add_fusion.3), channel_id=1, source_target_pairs={{0,48},{16,0},{32,16},{48,32},{1,49},{17,1},{33,17},{49,33},{2,50}... | collective-permute-start | bytes 5192 | tf_op jit(solution)/shard_map/ppermute | solution.py:400
  21.4 0.6 collective-permute-start
  24.6 0.7 collective-permute-done.1
  25.6 10.8 %all-to-all-done = bf16[16,320,128]{2,1,0:T(8,128)(2,1)S(1)} async-done(((bf16[16,320,128]{2,1,0:T(8,128)(2,1)}), bf16[16,320,128]{2,1,0:T(8,128)(2,1)S(1)}, u32[]{:S(2)}, u32[]{:S(2)}) %all-to-all-start) | async-done | bytes 1310752 | tf_op jit(solution)/shard_map/all_to_all | solution.py:433
  36.5 1.1 copy-done.7
  37.6 1.3 collective-permute-start.4
  38.9 1.5 %collective-permute-start.5 = (bf16[16,128,128]{2,1,0:T(8,128)(2,1)S(1)}, bf16[16,128,128]{2,1,0:T(8,128)(2,1)S(1)}, u32[]{:S(2)}, u32[]{:S(2)}) collective-permute-start(bf16[16,128,128]{2,1,0:T(8,128)(2,1)S(1)} %slice.29.refs_0_), channel_id=1, source_target_pairs={{0,48},{16,0},{32,16},{48,32},{1,49},{17,1},{33,17},{49,33},{2,50}... | collective-permute-start | bytes 1572872 | tf_op jit(solution)/shard_map/ppermute | solution.py:438
  40.5 1.2 slice.28.kv0
  42.1 1.8 %select_reduce_fusion.1 = s32[4,16,26]{1,2,0:T(8,128)S(1)} fusion(s32[4,16,26]{2,1,0:T(8,128)S(1)} %copy.16, pred[26,26]{1,0:T(8,128)(4,1)S(1)} %iota_compare_fusion.2), kind=kLoop, calls=%fused_computation.2 | loop fusion | flops 84864 | bytes 13988 | tf_op jit(solution)/shard_map/reduce_sum | solution.py:409
  44.5 7.8 %collective-permute-done.4.refs_1_ = bf16[16,128,128]{2,1,0:T(8,128)(2,1)S(1)} collective-permute-done((bf16[16,128,128]{2,1,0:T(8,128)(2,1)S(1)}, bf16[16,128,128]{2,1,0:T(8,128)(2,1)S(1)}, u32[]{:S(2)}, u32[]{:S(2)}) %collective-permute-start.4) | collective-permute-done | bytes 524320 | tf_op jit(solution)/shard_map/ppermute | solution.py:437
  52.4 2.7 %collective-permute-start.7 = (bf16[8,128,128]{2,1,0:T(8,128)(2,1)S(1)}, bf16[8,128,128]{2,1,0:T(8,128)(2,1)S(1)}, u32[]{:S(2)}, u32[]{:S(2)}) collective-permute-start(bf16[8,128,128]{2,1,0:T(8,128)(2,1)S(1)} %slice.31), channel_id=1, source_target_pairs={{0,48},{16,0},{32,16},{48,32},{1,49},{17,1},{33,17},{49,33},{2,50}... | collective-permute-start | bytes 786440 | tf_op jit(solution)/shard_map/ppermute | solution.py:440
  55.1 0.6 select_reduce_fusion
  55.8 4.4 %collective-permute-done.3.kv1 = bf16[16,192,128]{2,1,0:T(8,128)(2,1)S(1)} collective-permute-done((bf16[16,192,128]{2,1,0:T(8,128)(2,1)S(1)}, bf16[16,192,128]{2,1,0:T(8,128)(2,1)S(1)}, u32[]{:S(2)}, u32[]{:S(2)}) %collective-permute-start.3) | collective-permute-done | bytes 786464 | tf_op jit(solution)/shard_map/ppermute | solution.py:436
  60.2 16.3 %shard_map.100 = bf16[4,16,72,128]{3,2,1,0:T(8,128)(2,1)S(1)} custom-call(s32[4,216]{1,0:T(4,128)S(1)} %fusion.13.items, s32[4]{0:T(128)S(1)} %get-tuple-element.17.cnt, s32[4]{0:T(128)S(1)} %and_select_fusion.info, bf16[16,192,128]{2,1,0:T(8,128)(2,1)S(1)} %slice.28.kv0, bf16[16,192,128]{2,1,0:T(8,128)(2,1)S(1)} %collective-permute-done.3.kv1, ...), custom_call_target="tpu_custom_call" | custom-call | tf_op jit(solution)/shard_map/pallas_call | solution.py:224
  76.5 7.3 %shard_map.101 = bf16[1,16,72,128]{3,2,1,0:T(8,128)(2,1)S(1)} custom-call(s32[4,216]{1,0:T(4,128)S(1)} %fusion.13.items, s32[4]{0:T(128)S(1)} %get-tuple-element.17.cnt, s32[4]{0:T(128)S(1)} %and_select_fusion.info, bf16[16,192,128]{2,1,0:T(8,128)(2,1)S(1)} %slice.28.kv0, bf16[16,192,128]{2,1,0:T(8,128)(2,1)S(1)} %collective-permute-done.3.kv1, ...), custom_call_target="tpu_custom_call" | custom-call | tf_op jit(solution)/shard_map/pallas_call | solution.py:224
  83.9 26.2 %all_to_all.10.r_ref = bf16[64,72,128]{2,1,0:T(8,128)(2,1)S(1)} all-to-all(bf16[64,72,128]{2,1,0:T(8,128)(2,1)S(1)} %bitcast.13), channel_id=1, replica_groups=mesh['z'=2,'x'=4,'head'=16] {'x','head'}, dimensions={0} | all-to-all | bytes 2359296 | tf_op jit(solution)/shard_map/all_to_all | solution.py:445
  110.1 2.8 %mix.1 = (bf16[128,256]{1,0:T(8,128)(2,1)S(1)}, bf16[64,256]{1,0:T(8,128)(2,1)S(1)}, bf16[64,256]{1,0:T(8,128)(2,1)S(1)}) custom-call(bf16[64,72,128]{2,1,0:T(8,128)(2,1)S(1)} %all_to_all.10.r_ref, f32[128,1024]{1,0:T(8,128)S(1)} %bitcast.16, f32[1024,1024]{1,0:T(8,128)S(1)} %copy-done, f32[1,1024]{1,0:T(1,128)S(1)} %bitcast.17, f32[1024,256]{1,0:T(8,128)S(1)} %copy-done.4), custom_call_target="tpu_custom_call" | custom-call | tf_op jit(solution)/shard_map/mix/pallas_call | solution.py:285
  112.9 6.1 %collective-permute-start.8 = (bf16[64,256]{1,0:T(8,128)(2,1)S(1)}, bf16[64,256]{1,0:T(8,128)(2,1)S(1)}, u32[]{:S(2)}, u32[]{:S(2)}) collective-permute-start(bf16[64,256]{1,0:T(8,128)(2,1)S(1)} %get-tuple-element.15), channel_id=1, source_target_pairs={{0,1},{1,2},{2,3},{3,4},{4,5},{5,6},{6,7},{7,8},{8,9},{9,10},{10,1... | collective-permute-start | bytes 98312 | tf_op jit(solution)/shard_map/ppermute | solution.py:449
  119.1 1.9 %collective-permute-start.9 = (bf16[64,256]{1,0:T(8,128)(2,1)S(1)}, bf16[64,256]{1,0:T(8,128)(2,1)S(1)}, u32[]{:S(2)}, u32[]{:S(2)}) collective-permute-start(bf16[64,256]{1,0:T(8,128)(2,1)S(1)} %get-tuple-element.16), channel_id=1, source_target_pairs={{1,0},{2,1},{3,2},{4,3},{5,4},{6,5},{7,6},{8,7},{9,8},{10,9},{11,1... | collective-permute-start | bytes 98312 | tf_op jit(solution)/shard_map/ppermute | solution.py:450
  121.0 5.7 %collective-permute-done.9.below_ref = bf16[64,256]{1,0:T(8,128)(2,1)S(1)} collective-permute-done((bf16[64,256]{1,0:T(8,128)(2,1)S(1)}, bf16[64,256]{1,0:T(8,128)(2,1)S(1)}, u32[]{:S(2)}, u32[]{:S(2)}) %collective-permute-start.9) | collective-permute-done | bytes 32800 | tf_op jit(solution)/shard_map/ppermute | solution.py:450
  126.7 1.6 %copy-done.3 = bf16[256,4096]{1,0:T(8,128)(2,1)S(1)} copy-done((bf16[256,4096]{1,0:T(8,128)(2,1)S(1)}, bf16[256,4096]{1,0:T(8,128)(2,1)}, u32[]{:S(2)}) %copy-start.3) | copy-done | bytes 2097176
  128.3 12.0 %dense_head.1 = bf16[2,8,128,256]{3,2,1,0:T(8,128)(2,1)} custom-call(s32[1]{0:T(128)} %bitcast.pos, bf16[128,256]{1,0:T(8,128)(2,1)S(1)} %get-tuple-element.14.feat_ref, bf16[64,256]{1,0:T(8,128)(2,1)S(1)} %collective-permute-done.8.above_ref, bf16[64,256]{1,0:T(8,128)(2,1)S(1)} %collective-permute-done.9.below_ref, bf16[256,4096]{1,0:T(8,128)(2,1)S(1)} %copy-done.3, ...), custom_call_target="tpu_custom_call" | custom-call | tf_op jit(solution)/shard_map/dense_head/pallas_call | solution.py:372
  (51 shorter events, 3.0 us)
Async XLA Ops:
  10.4 7.9 %copy-start.8 = (s32[16,26]{1,0:T(8,128)S(1)}, s32[16,26]{1,0:T(8,128)}, u32[]{:S(2)}) copy-start(s32[16,26]{1,0:T(8,128)} %param.18) | copy-start | bytes 4996
  10.4 8.0 %copy-start.9 = (s32[16]{0:T(128)S(1)}, s32[16]{0:T(128)}, u32[]{:S(2)}) copy-start(s32[16]{0:T(128)} %param.19) | copy-start | bytes 196
  10.4 26.1 %all-to-all-start = ((bf16[16,320,128]{2,1,0:T(8,128)(2,1)}), bf16[16,320,128]{2,1,0:T(8,128)(2,1)S(1)}, u32[]{:S(2)}, u32[]{:S(2)}) async-start(bf16[16,320,128]{2,1,0:T(8,128)(2,1)} %qkv.1), calls=%async_computation | async-start | bytes 2621440 | tf_op jit(solution)/shard_map/all_to_all | solution.py:433
  18.4 6.3 %collective-permute-start.2 = (s32[16,27]{0,1:T(8,128)S(1)}, s32[16,27]{0,1:T(8,128)S(1)}, u32[]{:S(2)}, u32[]{:S(2)}) collective-permute-start(s32[16,27]{0,1:T(8,128)S(1)} %pad_add_fusion.3), channel_id=1, source_target_pairs={{0,48},{16,0},{32,16},{48,32},{1,49},{17,1},{33,17},{49,33},{2,50}... | collective-permute-start | bytes 5192 | tf_op jit(solution)/shard_map/ppermute | solution.py:400
  20.9 4.4 %collective-permute-start.1 = (s32[16,27]{0,1:T(8,128)S(1)}, s32[16,27]{0,1:T(8,128)S(1)}, u32[]{:S(2)}, u32[]{:S(2)}) collective-permute-start(s32[16,27]{0,1:T(8,128)S(1)} %pad_add_fusion.3), channel_id=1, source_target_pairs={{0,32},{16,48},{32,0},{48,16},{1,33},{17,49},{33,1},{49,17},{2,34}... | collective-permute-start | bytes 5192 | tf_op jit(solution)/shard_map/ppermute | solution.py:400
  21.4 4.1 %collective-permute-start = (s32[16,27]{0,1:T(8,128)S(1)}, s32[16,27]{0,1:T(8,128)S(1)}, u32[]{:S(2)}, u32[]{:S(2)}) collective-permute-start(s32[16,27]{0,1:T(8,128)S(1)} %pad_add_fusion.3), channel_id=1, source_target_pairs={{0,16},{16,32},{32,48},{48,0},{1,17},{17,33},{33,49},{49,1},{2,18}... | collective-permute-start | bytes 5192 | tf_op jit(solution)/shard_map/ppermute | solution.py:400
  36.5 1.1 copy-start.7
  37.6 14.6 %collective-permute-start.4 = (bf16[16,128,128]{2,1,0:T(8,128)(2,1)S(1)}, bf16[16,128,128]{2,1,0:T(8,128)(2,1)S(1)}, u32[]{:S(2)}, u32[]{:S(2)}) collective-permute-start(bf16[16,128,128]{2,1,0:T(8,128)(2,1)S(1)} %slice.29.refs_0_), channel_id=1, source_target_pairs={{0,16},{16,32},{32,48},{48,0},{1,17},{17,33},{33,49},{49,1},{2,18}... | collective-permute-start | bytes 1572872 | tf_op jit(solution)/shard_map/ppermute | solution.py:437
  38.9 13.5 %collective-permute-start.5 = (bf16[16,128,128]{2,1,0:T(8,128)(2,1)S(1)}, bf16[16,128,128]{2,1,0:T(8,128)(2,1)S(1)}, u32[]{:S(2)}, u32[]{:S(2)}) collective-permute-start(bf16[16,128,128]{2,1,0:T(8,128)(2,1)S(1)} %slice.29.refs_0_), channel_id=1, source_target_pairs={{0,48},{16,0},{32,16},{48,32},{1,49},{17,1},{33,17},{49,33},{2,50}... | collective-permute-start | bytes 1572872 | tf_op jit(solution)/shard_map/ppermute | solution.py:438
  41.7 18.5 %collective-permute-start.3 = (bf16[16,192,128]{2,1,0:T(8,128)(2,1)S(1)}, bf16[16,192,128]{2,1,0:T(8,128)(2,1)S(1)}, u32[]{:S(2)}, u32[]{:S(2)}) collective-permute-start(bf16[16,192,128]{2,1,0:T(8,128)(2,1)S(1)} %slice.28.kv0), channel_id=1, source_target_pairs={{0,64},{64,0},{1,65},{65,1},{2,66},{66,2},{3,67},{67,3},{4,68},{68... | collective-permute-start | bytes 2359304 | tf_op jit(solution)/shard_map/ppermute | solution.py:436
  52.3 24.2 %collective-permute-start.6 = (bf16[8,128,128]{2,1,0:T(8,128)(2,1)S(1)}, bf16[8,128,128]{2,1,0:T(8,128)(2,1)S(1)}, u32[]{:S(2)}, u32[]{:S(2)}) collective-permute-start(bf16[8,128,128]{2,1,0:T(8,128)(2,1)S(1)} %slice.30), channel_id=1, source_target_pairs={{0,16},{16,32},{32,48},{48,0},{1,17},{17,33},{33,49},{49,1},{2,18}... | collective-permute-start | bytes 786440 | tf_op jit(solution)/shard_map/ppermute | solution.py:439
  52.4 24.1 %collective-permute-start.7 = (bf16[8,128,128]{2,1,0:T(8,128)(2,1)S(1)}, bf16[8,128,128]{2,1,0:T(8,128)(2,1)S(1)}, u32[]{:S(2)}, u32[]{:S(2)}) collective-permute-start(bf16[8,128,128]{2,1,0:T(8,128)(2,1)S(1)} %slice.31), channel_id=1, source_target_pairs={{0,48},{16,0},{32,16},{48,32},{1,49},{17,1},{33,17},{49,33},{2,50}... | collective-permute-start | bytes 786440 | tf_op jit(solution)/shard_map/ppermute | solution.py:440
  60.2 49.9 %copy-start.4 = (f32[1024,256]{1,0:T(8,128)S(1)}, f32[1024,256]{1,0:T(8,128)}, u32[]{:S(2)}) copy-start(f32[1024,256]{1,0:T(8,128)} %proj_ref.1) | copy-start | bytes 3145732
  76.5 33.6 %copy-start = (f32[1024,1024]{1,0:T(8,128)S(1)}, f32[1024,1024]{1,0:T(8,128)}, u32[]{:S(2)}) copy-start(f32[1024,1024]{1,0:T(8,128)} %w_ref.3) | copy-start | bytes 12582916
  83.8 26.3 %copy-start.2 = (f32[2,64,1024]{2,1,0:T(8,128)S(1)}, f32[2,64,1024]{2,1,0:T(8,128)}, u32[]{:S(2)}) copy-start(f32[2,64,1024]{2,1,0:T(8,128)} %param.10) | copy-start | bytes 1572868
  83.8 26.3 %copy-start.5 = (f32[1024]{0:T(1024)S(1)}, f32[1024]{0:T(1024)}, u32[]{:S(2)}) copy-start(f32[1024]{0:T(1024)} %param.13) | copy-start | bytes 12292
  110.1 16.6 %copy-start.1 = (bf16[2,3,3,256,256]{4,3,2,1,0:T(8,128)(2,1)S(1)}, bf16[2,3,3,256,256]{4,3,2,1,0:T(8,128)(2,1)}, u32[]{:S(2)}) copy-start(bf16[2,3,3,256,256]{4,3,2,1,0:T(8,128)(2,1)} %param.16) | copy-start | bytes 7077892
  110.1 16.6 %copy-start.6 = (f32[2,256]{1,0:T(2,128)S(1)}, f32[2,256]{1,0:T(2,128)}, u32[]{:S(2)}) copy-start(f32[2,256]{1,0:T(2,128)} %cb_ref.1) | copy-start | bytes 6148
  112.9 8.1 %collective-permute-start.8 = (bf16[64,256]{1,0:T(8,128)(2,1)S(1)}, bf16[64,256]{1,0:T(8,128)(2,1)S(1)}, u32[]{:S(2)}, u32[]{:S(2)}) collective-permute-start(bf16[64,256]{1,0:T(8,128)(2,1)S(1)} %get-tuple-element.15), channel_id=1, source_target_pairs={{0,1},{1,2},{2,3},{3,4},{4,5},{5,6},{6,7},{7,8},{8,9},{9,10},{10,1... | collective-permute-start | bytes 98312 | tf_op jit(solution)/shard_map/ppermute | solution.py:449
  119.1 7.6 %collective-permute-start.9 = (bf16[64,256]{1,0:T(8,128)(2,1)S(1)}, bf16[64,256]{1,0:T(8,128)(2,1)S(1)}, u32[]{:S(2)}, u32[]{:S(2)}) collective-permute-start(bf16[64,256]{1,0:T(8,128)(2,1)S(1)} %get-tuple-element.16), channel_id=1, source_target_pairs={{1,0},{2,1},{3,2},{4,3},{5,4},{6,5},{7,6},{8,7},{9,8},{10,9},{11,1... | collective-permute-start | bytes 98312 | tf_op jit(solution)/shard_map/ppermute | solution.py:450
  126.7 1.6 %copy-start.3 = (bf16[256,4096]{1,0:T(8,128)(2,1)S(1)}, bf16[256,4096]{1,0:T(8,128)(2,1)}, u32[]{:S(2)}) copy-start(bf16[256,4096]{1,0:T(8,128)(2,1)} %up_ref.1) | copy-start | bytes 6291460

commit v2 on v1

--- a/solution.py
+++ b/solution.py
@@ -46,7 +46,7 @@
 
     wh, wl = split(w_ref[...])
     r = dot3(xh[...], xl[...], wh, wl)
-    for u in range(2):
+    for u in range(4):
         q = r[:, u * 192 : u * 192 + HD] * 0.125
         k = r[:, u * 192 + HD : u * 192 + 2 * HD]
         v = r[:, u * 192 + 2 * HD : u * 192 + 3 * HD]
@@ -59,12 +59,12 @@
 def qkv(x, w):
     return pl.pallas_call(
         qkv_body,
-        grid=(HEADS // 2,),
+        grid=(HEADS // 4,),
         in_specs=[
             pl.BlockSpec((128, D), lambda g: (0, 0)),
-            pl.BlockSpec((D, 384), lambda g: (0, g)),
+            pl.BlockSpec((D, 768), lambda g: (0, g)),
         ],
-        out_specs=pl.BlockSpec((2, 320, 128), lambda g: (g, 0, 0)),
+        out_specs=pl.BlockSpec((4, 320, 128), lambda g: (g, 0, 0)),
         out_shape=jax.ShapeDtypeStruct((HEADS, 320, 128), bf16),
         scratch_shapes=[pltpu.VMEM((128, D), bf16), pltpu.VMEM((128, D), bf16)],
         name="qkv",

time: 141 us -> 138 us (0.979)
  Pallas kernels: 48.7 us -> 46.4 us
    pallas_call x1, Pallas kernels: 10.4 us -> 8.03 us  [qkv(): pl.pallas_call(qkv_body, grid=(HEADS // 4,), in_specs=[pl.BlockSpec((128,...]
where the time goes in v2:
time: 138 us
  Pallas kernels  46.4 us (34%)
  waiting for transfers between devices  29.6 us (21%)
  blocking collectives  26.2 us (19%)
  starting transfers between devices  25.3 us (18%)
  local copies, waits for them, and re-layouts  5.17 us (4%)
  other arithmetic  3.09 us (2%)
  between operations  2.19 us (2%)
    all_to_all x1, blocking collectives, on_device(): lax.all_to_all(part.reshape(64, 72, 128), ('x', 'head'), split_axis=0, co...  26.2 us
    pallas_call x2, Pallas kernels, attend(): pl.pallas_call(functools.partial(attend_body, sets), in_specs=[smem, smem...  23.6 us
    pallas_call x1, Pallas kernels, dense_head(): pl.pallas_call(head_body, grid=(2,), in_specs=[pl.BlockSpec(memory_space=...  12 us
    all_to_all x1, waiting for transfers between devices, on_device(): lax.all_to_all(packed, 'head', split_axis=0, concat_axis=0, tiled=True)  10.8 us
    pallas_call x1, Pallas kernels, qkv(): pl.pallas_call(qkv_body, grid=(HEADS // 4,), in_specs=[pl.BlockSpec((128,...  8.03 us
    all_to_all x1, starting transfers between devices, on_device(): lax.all_to_all(packed, 'head', split_axis=0, concat_axis=0, tiled=True)  7.87 us
    ppermute x1, waiting for transfers between devices, on_device(): q1 = lax.ppermute(q, 'x', right)  7.75 us
    ppermute x1, starting transfers between devices, on_device(): above = lax.ppermute(bot, 'head', [(i, i + 1) for i in range(15)])  6.13 us
  transfers between devices with their start and end apart: 11, of which 6 were waited for; matrix products, arithmetic and copies ran while one was open for 4% of the time, Pallas kernels for 12%

profile of v2, /device:TPU:97, one launch (start us, length us, event | category | flops | bytes accessed | tf_op | source)
XLA Modules:
  0.0 137.9 jit_solution(13871876615013732256)
XLA Ops:
  0.0 8.0 %qkv.1 = bf16[16,320,128]{2,1,0:T(8,128)(2,1)} custom-call(f32[128,1024]{1,0:T(8,128)} %bitcast.15, f32[1024,3072]{1,0:T(8,128)} %w_ref.2), custom_call_target="tpu_custom_call" | custom-call | tf_op jit(solution)/shard_map/qkv/pallas_call | solution.py:60
  8.0 7.9 %all-to-all-start = ((bf16[16,320,128]{2,1,0:T(8,128)(2,1)}), bf16[16,320,128]{2,1,0:T(8,128)(2,1)S(1)}, u32[]{:S(2)}, u32[]{:S(2)}) async-start(bf16[16,320,128]{2,1,0:T(8,128)(2,1)} %qkv.1), calls=%async_computation | async-start | bytes 2621440 | tf_op jit(solution)/shard_map/all_to_all | solution.py:433
  16.0 2.5 %collective-permute-start.2 = (s32[16,27]{0,1:T(8,128)S(1)}, s32[16,27]{0,1:T(8,128)S(1)}, u32[]{:S(2)}, u32[]{:S(2)}) collective-permute-start(s32[16,27]{0,1:T(8,128)S(1)} %pad_add_fusion.3), channel_id=1, source_target_pairs={{0,48},{16,0},{32,16},{48,32},{1,49},{17,1},{33,17},{49,33},{2,50}... | collective-permute-start | bytes 5192 | tf_op jit(solution)/shard_map/ppermute | solution.py:400
  19.1 0.6 collective-permute-start
  22.3 0.7 collective-permute-done.1
  23.3 10.8 %all-to-all-done = bf16[16,320,128]{2,1,0:T(8,128)(2,1)S(1)} async-done(((bf16[16,320,128]{2,1,0:T(8,128)(2,1)}), bf16[16,320,128]{2,1,0:T(8,128)(2,1)S(1)}, u32[]{:S(2)}, u32[]{:S(2)}) %all-to-all-start) | async-done | bytes 1310752 | tf_op jit(solution)/shard_map/all_to_all | solution.py:433
  34.1 1.1 copy-done.7
  35.3 1.3 collective-permute-start.4
  36.5 1.5 %collective-permute-start.5 = (bf16[16,128,128]{2,1,0:T(8,128)(2,1)S(1)}, bf16[16,128,128]{2,1,0:T(8,128)(2,1)S(1)}, u32[]{:S(2)}, u32[]{:S(2)}) collective-permute-start(bf16[16,128,128]{2,1,0:T(8,128)(2,1)S(1)} %slice.29.refs_0_), channel_id=1, source_target_pairs={{0,48},{16,0},{32,16},{48,32},{1,49},{17,1},{33,17},{49,33},{2,50}... | collective-permute-start | bytes 1572872 | tf_op jit(solution)/shard_map/ppermute | solution.py:438
  38.1 1.2 slice.28.kv0
  39.8 1.8 %select_reduce_fusion.1 = s32[4,16,26]{1,2,0:T(8,128)S(1)} fusion(s32[4,16,26]{2,1,0:T(8,128)S(1)} %copy.16, pred[26,26]{1,0:T(8,128)(4,1)S(1)} %iota_compare_fusion.2), kind=kLoop, calls=%fused_computation.2 | loop fusion | flops 84864 | bytes 13988 | tf_op jit(solution)/shard_map/reduce_sum | solution.py:409
  42.2 7.8 %collective-permute-done.4.refs_1_ = bf16[16,128,128]{2,1,0:T(8,128)(2,1)S(1)} collective-permute-done((bf16[16,128,128]{2,1,0:T(8,128)(2,1)S(1)}, bf16[16,128,128]{2,1,0:T(8,128)(2,1)S(1)}, u32[]{:S(2)}, u32[]{:S(2)}) %collective-permute-start.4) | collective-permute-done | bytes 524320 | tf_op jit(solution)/shard_map/ppermute | solution.py:437
  50.1 2.7 %collective-permute-start.7 = (bf16[8,128,128]{2,1,0:T(8,128)(2,1)S(1)}, bf16[8,128,128]{2,1,0:T(8,128)(2,1)S(1)}, u32[]{:S(2)}, u32[]{:S(2)}) collective-permute-start(bf16[8,128,128]{2,1,0:T(8,128)(2,1)S(1)} %slice.31), channel_id=1, source_target_pairs={{0,48},{16,0},{32,16},{48,32},{1,49},{17,1},{33,17},{49,33},{2,50}... | collective-permute-start | bytes 786440 | tf_op jit(solution)/shard_map/ppermute | solution.py:440
  52.8 0.6 select_reduce_fusion
  53.5 4.4 %collective-permute-done.3.kv1 = bf16[16,192,128]{2,1,0:T(8,128)(2,1)S(1)} collective-permute-done((bf16[16,192,128]{2,1,0:T(8,128)(2,1)S(1)}, bf16[16,192,128]{2,1,0:T(8,128)(2,1)S(1)}, u32[]{:S(2)}, u32[]{:S(2)}) %collective-permute-start.3) | collective-permute-done | bytes 786464 | tf_op jit(solution)/shard_map/ppermute | solution.py:436
  57.8 16.3 %shard_map.100 = bf16[4,16,72,128]{3,2,1,0:T(8,128)(2,1)S(1)} custom-call(s32[4,216]{1,0:T(4,128)S(1)} %fusion.13.items, s32[4]{0:T(128)S(1)} %get-tuple-element.17.cnt, s32[4]{0:T(128)S(1)} %and_select_fusion.info, bf16[16,192,128]{2,1,0:T(8,128)(2,1)S(1)} %slice.28.kv0, bf16[16,192,128]{2,1,0:T(8,128)(2,1)S(1)} %collective-permute-done.3.kv1, ...), custom_call_target="tpu_custom_call" | custom-call | tf_op jit(solution)/shard_map/pallas_call | solution.py:224
  74.1 7.3 %shard_map.101 = bf16[1,16,72,128]{3,2,1,0:T(8,128)(2,1)S(1)} custom-call(s32[4,216]{1,0:T(4,128)S(1)} %fusion.13.items, s32[4]{0:T(128)S(1)} %get-tuple-element.17.cnt, s32[4]{0:T(128)S(1)} %and_select_fusion.info, bf16[16,192,128]{2,1,0:T(8,128)(2,1)S(1)} %slice.28.kv0, bf16[16,192,128]{2,1,0:T(8,128)(2,1)S(1)} %collective-permute-done.3.kv1, ...), custom_call_target="tpu_custom_call" | custom-call | tf_op jit(solution)/shard_map/pallas_call | solution.py:224
  81.5 26.2 %all_to_all.10.r_ref = bf16[64,72,128]{2,1,0:T(8,128)(2,1)S(1)} all-to-all(bf16[64,72,128]{2,1,0:T(8,128)(2,1)S(1)} %bitcast.13), channel_id=1, replica_groups=mesh['z'=2,'x'=4,'head'=16] {'x','head'}, dimensions={0} | all-to-all | bytes 2359296 | tf_op jit(solution)/shard_map/all_to_all | solution.py:445
  107.8 2.8 %mix.1 = (bf16[128,256]{1,0:T(8,128)(2,1)S(1)}, bf16[64,256]{1,0:T(8,128)(2,1)S(1)}, bf16[64,256]{1,0:T(8,128)(2,1)S(1)}) custom-call(bf16[64,72,128]{2,1,0:T(8,128)(2,1)S(1)} %all_to_all.10.r_ref, f32[128,1024]{1,0:T(8,128)S(1)} %bitcast.16, f32[1024,1024]{1,0:T(8,128)S(1)} %copy-done, f32[1,1024]{1,0:T(1,128)S(1)} %bitcast.17, f32[1024,256]{1,0:T(8,128)S(1)} %copy-done.4), custom_call_target="tpu_custom_call" | custom-call | tf_op jit(solution)/shard_map/mix/pallas_call | solution.py:285
  110.6 6.1 %collective-permute-start.8 = (bf16[64,256]{1,0:T(8,128)(2,1)S(1)}, bf16[64,256]{1,0:T(8,128)(2,1)S(1)}, u32[]{:S(2)}, u32[]{:S(2)}) collective-permute-start(bf16[64,256]{1,0:T(8,128)(2,1)S(1)} %get-tuple-element.15), channel_id=1, source_target_pairs={{0,1},{1,2},{2,3},{3,4},{4,5},{5,6},{6,7},{7,8},{8,9},{9,10},{10,1... | collective-permute-start | bytes 98312 | tf_op jit(solution)/shard_map/ppermute | solution.py:449
  116.7 1.9 %collective-permute-start.9 = (bf16[64,256]{1,0:T(8,128)(2,1)S(1)}, bf16[64,256]{1,0:T(8,128)(2,1)S(1)}, u32[]{:S(2)}, u32[]{:S(2)}) collective-permute-start(bf16[64,256]{1,0:T(8,128)(2,1)S(1)} %get-tuple-element.16), channel_id=1, source_target_pairs={{1,0},{2,1},{3,2},{4,3},{5,4},{6,5},{7,6},{8,7},{9,8},{10,9},{11,1... | collective-permute-start | bytes 98312 | tf_op jit(solution)/shard_map/ppermute | solution.py:450
  118.7 5.7 %collective-permute-done.9.below_ref = bf16[64,256]{1,0:T(8,128)(2,1)S(1)} collective-permute-done((bf16[64,256]{1,0:T(8,128)(2,1)S(1)}, bf16[64,256]{1,0:T(8,128)(2,1)S(1)}, u32[]{:S(2)}, u32[]{:S(2)}) %collective-permute-start.9) | collective-permute-done | bytes 32800 | tf_op jit(solution)/shard_map/ppermute | solution.py:450
  124.4 1.6 %copy-done.3 = bf16[256,4096]{1,0:T(8,128)(2,1)S(1)} copy-done((bf16[256,4096]{1,0:T(8,128)(2,1)S(1)}, bf16[256,4096]{1,0:T(8,128)(2,1)}, u32[]{:S(2)}) %copy-start.3) | copy-done | bytes 2097176
  126.0 12.0 %dense_head.1 = bf16[2,8,128,256]{3,2,1,0:T(8,128)(2,1)} custom-call(s32[1]{0:T(128)} %bitcast.pos, bf16[128,256]{1,0:T(8,128)(2,1)S(1)} %get-tuple-element.14.feat_ref, bf16[64,256]{1,0:T(8,128)(2,1)S(1)} %collective-permute-done.8.above_ref, bf16[64,256]{1,0:T(8,128)(2,1)S(1)} %collective-permute-done.9.below_ref, bf16[256,4096]{1,0:T(8,128)(2,1)S(1)} %copy-done.3, ...), custom_call_target="tpu_custom_call" | custom-call | tf_op jit(solution)/shard_map/dense_head/pallas_call | solution.py:372
  (51 shorter events, 3.0 us)
Async XLA Ops:
  8.0 7.9 %copy-start.8 = (s32[16,26]{1,0:T(8,128)S(1)}, s32[16,26]{1,0:T(8,128)}, u32[]{:S(2)}) copy-start(s32[16,26]{1,0:T(8,128)} %param.18) | copy-start | bytes 4996
  8.0 8.0 %copy-start.9 = (s32[16]{0:T(128)S(1)}, s32[16]{0:T(128)}, u32[]{:S(2)}) copy-start(s32[16]{0:T(128)} %param.19) | copy-start | bytes 196
  8.0 26.1 %all-to-all-start = ((bf16[16,320,128]{2,1,0:T(8,128)(2,1)}), bf16[16,320,128]{2,1,0:T(8,128)(2,1)S(1)}, u32[]{:S(2)}, u32[]{:S(2)}) async-start(bf16[16,320,128]{2,1,0:T(8,128)(2,1)} %qkv.1), calls=%async_computation | async-start | bytes 2621440 | tf_op jit(solution)/shard_map/all_to_all | solution.py:433
  16.0 6.3 %collective-permute-start.2 = (s32[16,27]{0,1:T(8,128)S(1)}, s32[16,27]{0,1:T(8,128)S(1)}, u32[]{:S(2)}, u32[]{:S(2)}) collective-permute-start(s32[16,27]{0,1:T(8,128)S(1)} %pad_add_fusion.3), channel_id=1, source_target_pairs={{0,48},{16,0},{32,16},{48,32},{1,49},{17,1},{33,17},{49,33},{2,50}... | collective-permute-start | bytes 5192 | tf_op jit(solution)/shard_map/ppermute | solution.py:400
  18.6 4.4 %collective-permute-start.1 = (s32[16,27]{0,1:T(8,128)S(1)}, s32[16,27]{0,1:T(8,128)S(1)}, u32[]{:S(2)}, u32[]{:S(2)}) collective-permute-start(s32[16,27]{0,1:T(8,128)S(1)} %pad_add_fusion.3), channel_id=1, source_target_pairs={{0,32},{16,48},{32,0},{48,16},{1,33},{17,49},{33,1},{49,17},{2,34}... | collective-permute-start | bytes 5192 | tf_op jit(solution)/shard_map/ppermute | solution.py:400
  19.1 4.1 %collective-permute-start = (s32[16,27]{0,1:T(8,128)S(1)}, s32[16,27]{0,1:T(8,128)S(1)}, u32[]{:S(2)}, u32[]{:S(2)}) collective-permute-start(s32[16,27]{0,1:T(8,128)S(1)} %pad_add_fusion.3), channel_id=1, source_target_pairs={{0,16},{16,32},{32,48},{48,0},{1,17},{17,33},{33,49},{49,1},{2,18}... | collective-permute-start | bytes 5192 | tf_op jit(solution)/shard_map/ppermute | solution.py:400
  34.1 1.1 copy-start.7
  35.3 14.6 %collective-permute-start.4 = (bf16[16,128,128]{2,1,0:T(8,128)(2,1)S(1)}, bf16[16,128,128]{2,1,0:T(8,128)(2,1)S(1)}, u32[]{:S(2)}, u32[]{:S(2)}) collective-permute-start(bf16[16,128,128]{2,1,0:T(8,128)(2,1)S(1)} %slice.29.refs_0_), channel_id=1, source_target_pairs={{0,16},{16,32},{32,48},{48,0},{1,17},{17,33},{33,49},{49,1},{2,18}... | collective-permute-start | bytes 1572872 | tf_op jit(solution)/shard_map/ppermute | solution.py:437
  36.5 13.5 %collective-permute-start.5 = (bf16[16,128,128]{2,1,0:T(8,128)(2,1)S(1)}, bf16[16,128,128]{2,1,0:T(8,128)(2,1)S(1)}, u32[]{:S(2)}, u32[]{:S(2)}) collective-permute-start(bf16[16,128,128]{2,1,0:T(8,128)(2,1)S(1)} %slice.29.refs_0_), channel_id=1, source_target_pairs={{0,48},{16,0},{32,16},{48,32},{1,49},{17,1},{33,17},{49,33},{2,50}... | collective-permute-start | bytes 1572872 | tf_op jit(solution)/shard_map/ppermute | solution.py:438
  39.3 18.5 %collective-permute-start.3 = (bf16[16,192,128]{2,1,0:T(8,128)(2,1)S(1)}, bf16[16,192,128]{2,1,0:T(8,128)(2,1)S(1)}, u32[]{:S(2)}, u32[]{:S(2)}) collective-permute-start(bf16[16,192,128]{2,1,0:T(8,128)(2,1)S(1)} %slice.28.kv0), channel_id=1, source_target_pairs={{0,64},{64,0},{1,65},{65,1},{2,66},{66,2},{3,67},{67,3},{4,68},{68... | collective-permute-start | bytes 2359304 | tf_op jit(solution)/shard_map/ppermute | solution.py:436
  49.9 24.2 %collective-permute-start.6 = (bf16[8,128,128]{2,1,0:T(8,128)(2,1)S(1)}, bf16[8,128,128]{2,1,0:T(8,128)(2,1)S(1)}, u32[]{:S(2)}, u32[]{:S(2)}) collective-permute-start(bf16[8,128,128]{2,1,0:T(8,128)(2,1)S(1)} %slice.30), channel_id=1, source_target_pairs={{0,16},{16,32},{32,48},{48,0},{1,17},{17,33},{33,49},{49,1},{2,18}... | collective-permute-start | bytes 786440 | tf_op jit(solution)/shard_map/ppermute | solution.py:439
  50.1 24.1 %collective-permute-start.7 = (bf16[8,128,128]{2,1,0:T(8,128)(2,1)S(1)}, bf16[8,128,128]{2,1,0:T(8,128)(2,1)S(1)}, u32[]{:S(2)}, u32[]{:S(2)}) collective-permute-start(bf16[8,128,128]{2,1,0:T(8,128)(2,1)S(1)} %slice.31), channel_id=1, source_target_pairs={{0,48},{16,0},{32,16},{48,32},{1,49},{17,1},{33,17},{49,33},{2,50}... | collective-permute-start | bytes 786440 | tf_op jit(solution)/shard_map/ppermute | solution.py:440
  57.8 49.9 %copy-start.4 = (f32[1024,256]{1,0:T(8,128)S(1)}, f32[1024,256]{1,0:T(8,128)}, u32[]{:S(2)}) copy-start(f32[1024,256]{1,0:T(8,128)} %proj_ref.1) | copy-start | bytes 3145732
  74.1 33.6 %copy-start = (f32[1024,1024]{1,0:T(8,128)S(1)}, f32[1024,1024]{1,0:T(8,128)}, u32[]{:S(2)}) copy-start(f32[1024,1024]{1,0:T(8,128)} %w_ref.3) | copy-start | bytes 12582916
  81.5 26.3 %copy-start.2 = (f32[2,64,1024]{2,1,0:T(8,128)S(1)}, f32[2,64,1024]{2,1,0:T(8,128)}, u32[]{:S(2)}) copy-start(f32[2,64,1024]{2,1,0:T(8,128)} %param.10) | copy-start | bytes 1572868
  81.5 26.3 %copy-start.5 = (f32[1024]{0:T(1024)S(1)}, f32[1024]{0:T(1024)}, u32[]{:S(2)}) copy-start(f32[1024]{0:T(1024)} %param.13) | copy-start | bytes 12292
  107.8 16.6 %copy-start.1 = (bf16[2,3,3,256,256]{4,3,2,1,0:T(8,128)(2,1)S(1)}, bf16[2,3,3,256,256]{4,3,2,1,0:T(8,128)(2,1)}, u32[]{:S(2)}) copy-start(bf16[2,3,3,256,256]{4,3,2,1,0:T(8,128)(2,1)} %param.16) | copy-start | bytes 7077892
  107.8 16.6 %copy-start.6 = (f32[2,256]{1,0:T(2,128)S(1)}, f32[2,256]{1,0:T(2,128)}, u32[]{:S(2)}) copy-start(f32[2,256]{1,0:T(2,128)} %cb_ref.1) | copy-start | bytes 6148
  110.6 8.1 %collective-permute-start.8 = (bf16[64,256]{1,0:T(8,128)(2,1)S(1)}, bf16[64,256]{1,0:T(8,128)(2,1)S(1)}, u32[]{:S(2)}, u32[]{:S(2)}) collective-permute-start(bf16[64,256]{1,0:T(8,128)(2,1)S(1)} %get-tuple-element.15), channel_id=1, source_target_pairs={{0,1},{1,2},{2,3},{3,4},{4,5},{5,6},{6,7},{7,8},{8,9},{9,10},{10,1... | collective-permute-start | bytes 98312 | tf_op jit(solution)/shard_map/ppermute | solution.py:449
  116.7 7.6 %collective-permute-start.9 = (bf16[64,256]{1,0:T(8,128)(2,1)S(1)}, bf16[64,256]{1,0:T(8,128)(2,1)S(1)}, u32[]{:S(2)}, u32[]{:S(2)}) collective-permute-start(bf16[64,256]{1,0:T(8,128)(2,1)S(1)} %get-tuple-element.16), channel_id=1, source_target_pairs={{1,0},{2,1},{3,2},{4,3},{5,4},{6,5},{7,6},{8,7},{9,8},{10,9},{11,1... | collective-permute-start | bytes 98312 | tf_op jit(solution)/shard_map/ppermute | solution.py:450
  124.4 1.6 %copy-start.3 = (bf16[256,4096]{1,0:T(8,128)(2,1)S(1)}, bf16[256,4096]{1,0:T(8,128)(2,1)}, u32[]{:S(2)}) copy-start(bf16[256,4096]{1,0:T(8,128)(2,1)} %up_ref.1) | copy-start | bytes 6291460
